TPU v7x, 512 devices: a whole 4x8x8 slice. The times are simulated.
512 devices in a mesh: row: 8 (over z), col: 16 (over y, core), vox: 4 (over x).
Axes of the slice: x: 4, y: 8, z: 8, core: 2. Of those that a mesh axis runs over, the one named last changes fastest.
Arguments:
- panel_top: bfloat16 [1024, 1024], P('row', ('col', 'vox')), may hold values from -0.059814453 to 0.059814453
- panel_low: bfloat16 [8192, 1024], P('row', ('col', 'vox')), may hold values from -1.1953125 to 1.1953125
- panel_next: bfloat16 [8192, 1024], P('row', ('col', 'vox')), may hold values from -1.1953125 to 1.1953125
- gram_rest: bfloat16 [8192, 8192], P('row', ('col', 'vox')), may hold values from -18 to 18
- inverses: bfloat16 [2, 1024, 1024], P(None, 'row'), as said below
- right_top: bfloat16 [2, 1024, 8192], P(None, None, ('col', 'vox')), may hold values from -1.796875 to 1.796875
- right_low: bfloat16 [8192, 8192], P('row', ('col', 'vox')), may hold values from -24 to 24
Outputs:
- factor: bfloat16 [2, 8192, 1024], P(None, 'row', ('col', 'vox'))
- solved: bfloat16 [2, 1024, 8192], P(None, None, ('col', 'vox'))
- trailing: float32 [8192, 8192], P('row', ('col', 'vox'))
- residual: float32 [8192, 8192], P('row', ('col', 'vox'))
Inputs may be any that keep to these rules, and one draw needn't show every extreme that they name: Each inverses[k] is lower triangular with diagonal entries from 1 to 2.
All inputs are finite; a program needn't handle non-finite values.
Results may differ from a plain program's by a relative error of at most 0.0057.
Values may be sent and summed in bfloat16 or wider, within the bound.
No kernel may reach another device: no remote copies, remote signals or barrier semaphores. Data moves between devices by JAX's collectives and lax.ppermute only.
A program may use at most 64 MiB of HBM per device.

v0:
```python
import jax
import jax.numpy as jnp
from jax import lax
from jax.sharding import PartitionSpec as P


def spread(block, axis, source):
    block = jnp.where(lax.axis_index(axis) == source, block, jnp.zeros_like(block))
    return lax.psum(block, axis)


def contract(left, right):
    return lax.dot_general(
        left, right, (((1,), (1,)), ((), ())), preferred_element_type=jnp.float32
    )


def per_device(panel_top, panel_low, panel_next, gram_rest, inverses, right_top, right_low):
    col_index = lax.axis_index(("col", "vox"))
    row_index = lax.axis_index("row")
    col_width = panel_low.shape[1]
    top_rows = panel_top.shape[0]
    low_rows = panel_low.shape[0]
    rest_cols = gram_rest.shape[1]
    root_row = col_index * rest_cols // low_rows
    whole_inverses = lax.all_gather(inverses, "row", axis=1, tiled=True)
    own_rows = lax.dynamic_slice_in_dim(whole_inverses, col_index * col_width, col_width, 1)
    rows_used = own_rows[0]
    own_top = contract(lax.all_gather(panel_top, ("col", "vox"), axis=1, tiled=True), rows_used)
    own_low = contract(lax.all_gather(panel_low, ("col", "vox"), axis=1, tiled=True), rows_used)
    first_top, first_low = (
        lax.all_gather(own_top.astype(jnp.bfloat16), ("col", "vox"), axis=1, tiled=True),
        lax.all_gather(own_low.astype(jnp.bfloat16), ("col", "vox"), axis=1, tiled=True),
    )
    outgoing = (
        lax.dynamic_slice_in_dim(
            first_top, col_index * col_width - root_row * top_rows, col_width, 0
        ),
        lax.dynamic_slice_in_dim(
            first_low, col_index * rest_cols - root_row * low_rows, rest_cols, 0
        ),
    )
    owner_top, owner_low = (
        spread(outgoing[0], "row", root_row),
        spread(outgoing[1], "row", root_row),
    )
    updated = (panel_next.astype(jnp.float32) - contract(first_low, owner_top)).astype(jnp.bfloat16)
    rows_used = own_rows[1]
    own_next = contract(lax.all_gather(updated, ("col", "vox"), axis=1, tiled=True), rows_used)
    second_low = lax.all_gather(own_next.astype(jnp.bfloat16), ("col", "vox"), axis=1, tiled=True)
    owner_next = spread(
        lax.dynamic_slice_in_dim(
            second_low, col_index * rest_cols - root_row * low_rows, rest_cols, 0
        ),
        "row",
        root_row,
    )
    trailing = (
        gram_rest.astype(jnp.float32)
        - contract(first_low, owner_low)
        - contract(second_low, owner_next)
    )
    first_solve = jnp.dot(
        whole_inverses[0], right_top[0], preferred_element_type=jnp.float32
    ).astype(jnp.bfloat16)
    top_slice = lax.dynamic_slice_in_dim(right_top[1], row_index * top_rows, top_rows, 0)
    top_part = (
        top_slice.astype(jnp.float32)
        - jnp.dot(first_top, first_solve, preferred_element_type=jnp.float32)
    ).astype(jnp.bfloat16)
    top_new = lax.all_gather(top_part, "row", axis=0, tiled=True)
    second_solve = jnp.dot(whole_inverses[1], top_new, preferred_element_type=jnp.float32).astype(
        jnp.bfloat16
    )
    residual = (
        right_low.astype(jnp.float32)
        - jnp.dot(first_low, first_solve, preferred_element_type=jnp.float32)
        - jnp.dot(second_low, second_solve, preferred_element_type=jnp.float32)
    )
    factor = jnp.stack(
        [
            lax.dynamic_slice_in_dim(first_low, col_index * col_width, col_width, 1),
            lax.dynamic_slice_in_dim(second_low, col_index * col_width, col_width, 1),
        ]
    )
    solved = jnp.stack([first_solve, second_solve])
    return (factor, solved, trailing, residual)


def solution(mesh):
    in_specs = (
        P("row", ("col", "vox")),
        P("row", ("col", "vox")),
        P("row", ("col", "vox")),
        P("row", ("col", "vox")),
        P(None, "row", None),
        P(None, None, ("col", "vox")),
        P("row", ("col", "vox")),
    )
    out_specs = (
        P(None, "row", ("col", "vox")),
        P(None, None, ("col", "vox")),
        P("row", ("col", "vox")),
        P("row", ("col", "vox")),
    )
    return jax.shard_map(
        per_device, mesh=mesh, in_specs=in_specs, out_specs=out_specs, check_vma=False
    )
```

profile of v0, /device:TPU:2, one launch (start us, length us, event | category | flops | bytes accessed | tf_op | source)
XLA Modules:
  0.0 587.9 jit_solution(6978349543570293704)
XLA Ops:
  7.2 0.0 copy-start.7
  7.2 0.0 all-gather.8.cloned.1.call-start
  7.2 0.7 all-gather.8.cloned.1.call-update
  7.9 0.0 all-gather.6.cloned.1.call-start
  8.0 0.7 all-gather.6.cloned.1.call-update
  8.7 0.0 copy-start.6
  8.7 0.0 all-gather.10.cloned.1.call-start
  8.7 88.6 %all-gather.8.cloned.1.call-done = bf16[1024,1024]{0,1:T(8,128)(2,1)} async-done(((bf16[1024,16]{0,1:T(8,128)(2,1)}), bf16[1024,1024]{0,1:T(8,128)(2,1)}) %all-gather.8.cloned.1.call-update) | async-done | bytes 2097168 | tf_op jit(solution)/shard_map/all_gather | solution.py:30
  97.4 59.5 %all-gather.6.cloned.1.call-done = bf16[2,1024,1024]{2,1,0:T(8,128)(2,1)} async-done(((bf16[2,128,1024]{2,1,0:T(8,128)(2,1)}), bf16[2,1024,1024]{2,1,0:T(8,128)(2,1)}) %all-gather.6.cloned.1.call-update) | async-done | bytes 4194320 | tf_op jit(solution)/shard_map/all_gather | solution.py:26
  156.9 2.6 fusion.6
  159.5 0.0 all-gather.10.cloned.1.call-update
  159.5 0.0 all-gather.12.cloned.1.call-start
  159.6 0.0 copy-done.7
  159.6 69.7 %all_gather.27 = bf16[128,1024]{0,1:T(8,128)(2,1)S(1)} all-gather(bf16[128,16]{0,1:T(8,128)(2,1)S(1)} %copy-done.7), channel_id=1, replica_groups=mesh['row'=8,'col'=16,'vox'=4] {'col','vox'}, dimensions={1}, use_global_device_ids=true | all-gather | bytes 266240 | tf_op jit(solution)/shard_map/all_gather | solution.py:29
  229.3 0.9 fusion.7
  230.2 66.4 %all_gather.28 = bf16[128,1024]{0,1:T(8,128)(2,1)S(1)} all-gather(bf16[128,16]{0,1:T(8,128)(2,1)S(1)} %fusion.7), channel_id=1, replica_groups=mesh['row'=8,'col'=16,'vox'=4] {'col','vox'}, dimensions={1}, use_global_device_ids=true | all-gather | bytes 266240 | tf_op jit(solution)/shard_map/all_gather | solution.py:32
  296.6 0.1 dynamic-slice_select_fusion.2
  296.8 31.6 %psum.21 = bf16[16,1024]{0,1:T(8,128)(2,1)S(1)} all-reduce(bf16[16,1024]{0,1:T(8,128)(2,1)S(1)} %dynamic-slice_select_fusion.2), channel_id=1, replica_groups=mesh['row'=8,'col'=16,'vox'=4] {'row'}, use_global_device_ids=true, to_apply=%region_0.1 | all-reduce | flops 16384 | bytes 65536 | tf_op jit(solution)/shard_map/psum | solution.py:9
  328.3 0.0 copy-start.4
  328.4 0.0 all-gather.10.cloned.1.call-done
  328.4 0.0 copy-done.6
  328.4 2.7 fusion.4
  331.1 0.0 all-gather.12.cloned.1.call-update
  331.1 0.0 all-gather.14.cloned.1.call-start
  331.2 80.5 %all-gather.12.cloned.1.call-done = bf16[1024,1024]{0,1:T(8,128)(2,1)} async-done(((bf16[1024,16]{0,1:T(8,128)(2,1)}), bf16[1024,1024]{0,1:T(8,128)(2,1)}) %all-gather.12.cloned.1.call-update) | async-done | bytes 2097168 | tf_op jit(solution)/shard_map/all_gather | solution.py:49
  411.7 2.6 convolution_convert_fusion
  414.3 0.0 all-gather.14.cloned.1.call-update
  414.3 0.0 all-reduce.3.cloned.1.call-start
  414.4 0.0 slice-start
  414.4 0.0 copy-done.4
  414.4 0.0 copy-start.8
  414.4 2.4 fusion.2
  416.9 0.3 fusion.5
  417.2 26.8 %all_gather.31 = bf16[1024,128]{1,0:T(8,128)(2,1)S(1)} all-gather(bf16[128,128]{1,0:T(8,128)(2,1)S(1)} %fusion.5), channel_id=1, replica_groups=mesh['row'=8,'col'=16,'vox'=4] {'row'}, dimensions={0}, use_global_device_ids=true | all-gather | bytes 294912 | tf_op jit(solution)/shard_map/all_gather | solution.py:71
  444.0 0.7 fusion.3
  444.7 0.8 pad_maximum_fusion
  445.5 0.0 copy-done
  445.6 0.8 dynamic-slice_select_fusion.1
  446.3 0.7 convolution_subtract_fusion.1
  447.1 48.9 %all-gather.14.cloned.1.call-done = bf16[1024,1024]{0,1:T(8,128)(2,1)} async-done(((bf16[1024,16]{0,1:T(8,128)(2,1)}), bf16[1024,1024]{0,1:T(8,128)(2,1)}) %all-gather.14.cloned.1.call-update) | async-done | bytes 2097168 | tf_op jit(solution)/shard_map/all_gather | solution.py:50
  496.0 1.7 dynamic-slice_select_fusion
  497.7 0.0 all-reduce.3.cloned.1.call-update
  497.7 0.8 dynamic-slice_bitcast_fusion.3
  498.4 0.6 pad_maximum_fusion.1
  499.1 3.2 convolution_subtract_fusion
  502.3 75.4 %all-reduce.3.cloned.1.call-done = (bf16[128,1024]{0,1:T(8,128)(2,1)}, bf16[128,1024]{0,1:T(8,128)(2,1)}) async-done(((bf16[128,1024]{0,1:T(8,128)(2,1)}, bf16[128,1024]{0,1:T(8,128)(2,1)}), (bf16[128,1024]{0,1:T(8,128)(2,1)}, bf16[128,1024]{0,1:T(8,128)(2,1)})) %all-reduce.3.cloned.1.call-update) | async-done | bytes 524304 | tf_op jit(solution)/shard_map/psum | solution.py:9
  577.6 1.8 convolution_subtract_fusion.3
  579.5 1.5 convolution_subtract_fusion.2
  (12 shorter events, 0.0 us)
Async XLA Ops:
  7.2 152.4 %copy-start.7 = (bf16[128,16]{0,1:T(8,128)(2,1)S(1)}, bf16[128,16]{0,1:T(8,128)(2,1)}, u32[]{:S(2)}) copy-start(bf16[128,16]{0,1:T(8,128)(2,1)} %param.7) | copy-start | bytes 12292
  7.2 90.2 %all-gather.8.cloned.1.call-start = ((), (), s32[]{:S(2)}) async-start(), calls=%async_computation.1 | async-start | bytes 2129920 | tf_op jit(solution)/shard_map/all_gather | solution.py:30
  7.9 149.0 %all-gather.6.cloned.1.call-start = ((), (), s32[]{:S(2)}) async-start(), calls=%async_computation | async-start | bytes 4718592 | tf_op jit(solution)/shard_map/all_gather | solution.py:26
  8.7 319.7 %copy-start.6 = (bf16[1024,16]{0,1:T(8,128)(2,1)S(1)}, bf16[1024,16]{0,1:T(8,128)(2,1)}, u32[]{:S(2)}) copy-start(bf16[1024,16]{0,1:T(8,128)(2,1)} %param.9) | copy-start | bytes 98308
  8.7 319.7 %all-gather.10.cloned.1.call-start = ((), (), s32[]{:S(2)}) async-start(), calls=%async_computation.2 | async-start | bytes 2129920 | tf_op jit(solution)/shard_map/all_gather | solution.py:33
  159.5 252.2 %all-gather.12.cloned.1.call-start = ((), (), s32[]{:S(2)}) async-start(), calls=%async_computation.3 | async-start | bytes 2129920 | tf_op jit(solution)/shard_map/all_gather | solution.py:49
  328.3 86.1 %copy-start.4 = (bf16[2,1024,128]{2,1,0:T(8,128)(2,1)S(1)}, bf16[2,1024,128]{2,1,0:T(8,128)(2,1)}, u32[]{:S(2)}) copy-start(bf16[2,1024,128]{2,1,0:T(8,128)(2,1)} %param.12) | copy-start | bytes 1572868
  331.1 164.9 %all-gather.14.cloned.1.call-start = ((), (), s32[]{:S(2)}) async-start(), calls=%async_computation.4 | async-start | bytes 2129920 | tf_op jit(solution)/shard_map/all_gather | solution.py:50
  414.3 163.3 %all-reduce.3.cloned.1.call-start = ((), (), s32[]{:S(2)}) async-start(), calls=%async_computation.5 | async-start | bytes 1048576 | tf_op jit(solution)/shard_map/psum | solution.py:9
  414.4 2.5 slice-start
  414.4 29.5 %copy-start.8 = (bf16[2,1024,1024]{2,1,0:T(8,128)(2,1)S(1)}, bf16[2,1024,1024]{2,1,0:T(8,128)(2,1)}, u32[]{:S(2)}) copy-start(bf16[2,1024,1024]{2,1,0:T(8,128)(2,1)} %all-gather.6.cloned.1.call-done) | copy-start | bytes 12582916
  444.0 1.6 copy-start
  444.0 2.4 copy-start.2
  499.1 78.6 %copy-start.3 = (bf16[1024,128]{1,0:T(8,128)(2,1)S(1)}, bf16[1024,128]{1,0:T(8,128)(2,1)}, u32[]{:S(2)}) copy-start(bf16[1024,128]{1,0:T(8,128)(2,1)} %param.10) | copy-start | bytes 786436
  577.6 1.8 copy-start.1
  577.6 1.9 copy-start.5
Sparse Core Ops, SparseCore 0:
  11.4 85.9 all-gather.7
  99.5 57.3 all-gather.5
  160.8 79.4 all-gather.9
  331.2 80.4 all-gather.11
  415.5 80.4 all-gather.13
  498.8 78.8 all-reduce.2
where the time goes:
time: 588 us
  waiting for transfers between devices  354 us (60%)
  blocking collectives  194 us (33%)
  matrix products  19.5 us (3%)
  between operations  14.3 us (2%)
    all_gather x1, waiting for transfers between devices, per_device(): lax.all_gather(panel_low, ('col', 'vox'), axis=1, tiled=True)  88.6 us
    all_gather x1, waiting for transfers between devices, per_device(): lax.all_gather(updated, ('col', 'vox'), axis=1, tiled=True)  80.5 us
    psum x1, waiting for transfers between devices, spread(): return lax.psum(block, axis)  75.4 us
    all_gather x1, blocking collectives, per_device(): lax.all_gather(panel_top, ('col', 'vox'), axis=1, tiled=True)  69.7 us
    all_gather x1, blocking collectives, per_device(): lax.all_gather(own_top.astype(jnp.bfloat16), ('col', 'vox'), axis=1, tile...  66.4 us
    all_gather x1, waiting for transfers between devices, per_device(): whole_inverses = lax.all_gather(inverses, 'row', axis=1, tiled=True)  59.5 us
    all_gather x1, waiting for transfers between devices, per_device(): lax.all_gather(own_next.astype(jnp.bfloat16), ('col', 'vox'), axis=1, til...  48.9 us
    psum x1, blocking collectives, spread(): return lax.psum(block, axis)  31.6 us
  transfers between devices with their start and end apart: 6, of which 5 were waited for; matrix products, arithmetic and copies ran while one was open for 2% of the time, Pallas kernels for 0%

commit v1 on v0

--- a/solution.py
+++ b/solution.py
@@ -2,6 +2,14 @@
 import jax.numpy as jnp
 from jax import lax
 from jax.sharding import PartitionSpec as P
+
+
+def tiled_gather(array, axis, dim):
+    length = lax.axis_size(axis)
+    repeats = [length if d == dim else 1 for d in range(array.ndim)]
+    return lax.all_to_all(
+        jnp.tile(array, repeats), axis, split_axis=dim, concat_axis=dim, tiled=True
+    )
 
 
 def spread(block, axis, source):
@@ -46,7 +54,7 @@
     )
     updated = (panel_next.astype(jnp.float32) - contract(first_low, owner_top)).astype(jnp.bfloat16)
     rows_used = own_rows[1]
-    own_next = contract(lax.all_gather(updated, ("col", "vox"), axis=1, tiled=True), rows_used)
+    own_next = contract(tiled_gather(updated, ("col", "vox"), 1), rows_used)
     second_low = lax.all_gather(own_next.astype(jnp.bfloat16), ("col", "vox"), axis=1, tiled=True)
     owner_next = spread(
         lax.dynamic_slice_in_dim(

time: 588 us -> 564 us (0.959)
  waiting for transfers between devices: 354 us -> 321 us
  starting transfers between devices: 0.24 us -> 10.4 us
    all_gather x1 -> x0, waiting for transfers between devices: 80.5 us -> none  [per_device(): lax.all_gather(updated, ('col', 'vox'), axis=1, tiled=True)]
    all_to_all x0 -> x1, waiting for transfers between devices: none -> 51.2 us  [tiled_gather(): lax.all_to_all(jnp.tile(array, repeats), axis, split_axis=dim, concat_axi...]
    all_to_all x0 -> x1, starting transfers between devices: none -> 10.2 us  [tiled_gather(): lax.all_to_all(jnp.tile(array, repeats), axis, split_axis=dim, concat_axi...]
where the time goes in v1:
time: 564 us; the launch traced here: 563 us
  waiting for transfers between devices  321 us (57%)
  blocking collectives  193 us (34%)
  matrix products  18 us (3%)
  between operations  14 us (2%)
  starting transfers between devices  10.4 us (2%)
    all_gather x1, waiting for transfers between devices, per_device(): lax.all_gather(panel_low, ('col', 'vox'), axis=1, tiled=True)  88.6 us
    psum x1, waiting for transfers between devices, spread(): return lax.psum(block, axis)  75.4 us
    all_gather x1, blocking collectives, per_device(): lax.all_gather(panel_top, ('col', 'vox'), axis=1, tiled=True)  69.7 us
    all_gather x1, blocking collectives, per_device(): lax.all_gather(own_top.astype(jnp.bfloat16), ('col', 'vox'), axis=1, tile...  66.5 us
    all_gather x1, waiting for transfers between devices, per_device(): whole_inverses = lax.all_gather(inverses, 'row', axis=1, tiled=True)  59.5 us
    all_to_all x1, waiting for transfers between devices, tiled_gather(): lax.all_to_all(jnp.tile(array, repeats), axis, split_axis=dim, concat_axi...  51.2 us
    all_gather x1, waiting for transfers between devices, per_device(): lax.all_gather(own_next.astype(jnp.bfloat16), ('col', 'vox'), axis=1, til...  45.2 us
    psum x1, blocking collectives, spread(): return lax.psum(block, axis)  31.5 us
  transfers between devices with their start and end apart: 6, of which 5 were waited for; matrix products, arithmetic and copies ran while one was open for 2% of the time, Pallas kernels for 0%

profile of v1, /device:TPU:2, one launch (start us, length us, event | category | flops | bytes accessed | tf_op | source)
XLA Modules:
  0.0 563.0 jit_solution(18259317767120465705)
XLA Ops:
  7.2 0.0 copy-start.7
  7.2 0.0 all-gather.7.cloned.1.call-start
  7.2 0.7 all-gather.7.cloned.1.call-update
  7.9 0.0 all-gather.5.cloned.1.call-start
  8.0 0.7 all-gather.5.cloned.1.call-update
  8.7 0.0 copy-start.6
  8.7 0.0 all-gather.9.cloned.1.call-start
  8.7 88.6 %all-gather.7.cloned.1.call-done = bf16[1024,1024]{0,1:T(8,128)(2,1)} async-done(((bf16[1024,16]{0,1:T(8,128)(2,1)}), bf16[1024,1024]{0,1:T(8,128)(2,1)}) %all-gather.7.cloned.1.call-update) | async-done | bytes 2097168 | tf_op jit(solution)/shard_map/all_gather | solution.py:38
  97.4 59.5 %all-gather.5.cloned.1.call-done = bf16[2,1024,1024]{2,1,0:T(8,128)(2,1)} async-done(((bf16[2,128,1024]{2,1,0:T(8,128)(2,1)}), bf16[2,1024,1024]{2,1,0:T(8,128)(2,1)}) %all-gather.5.cloned.1.call-update) | async-done | bytes 4194320 | tf_op jit(solution)/shard_map/all_gather | solution.py:34
  156.9 2.6 fusion.6
  159.5 0.0 all-gather.9.cloned.1.call-update
  159.5 0.0 copy-done.7
  159.5 69.7 %all_gather.24 = bf16[128,1024]{0,1:T(8,128)(2,1)S(1)} all-gather(bf16[128,16]{0,1:T(8,128)(2,1)S(1)} %copy-done.7), channel_id=1, replica_groups=mesh['row'=8,'col'=16,'vox'=4] {'col','vox'}, dimensions={1}, use_global_device_ids=true | all-gather | bytes 266240 | tf_op jit(solution)/shard_map/all_gather | solution.py:37
  229.3 0.9 fusion.7
  230.2 66.5 %all_gather.25 = bf16[128,1024]{0,1:T(8,128)(2,1)S(1)} all-gather(bf16[128,16]{0,1:T(8,128)(2,1)S(1)} %fusion.7), channel_id=1, replica_groups=mesh['row'=8,'col'=16,'vox'=4] {'col','vox'}, dimensions={1}, use_global_device_ids=true | all-gather | bytes 266240 | tf_op jit(solution)/shard_map/all_gather | solution.py:40
  296.7 0.1 dynamic-slice_select_fusion.2
  296.8 31.5 %psum.21 = bf16[16,1024]{0,1:T(8,128)(2,1)S(1)} all-reduce(bf16[16,1024]{0,1:T(8,128)(2,1)S(1)} %dynamic-slice_select_fusion.2), channel_id=1, replica_groups=mesh['row'=8,'col'=16,'vox'=4] {'row'}, use_global_device_ids=true, to_apply=%region_0.1 | all-reduce | flops 16384 | bytes 65536 | tf_op jit(solution)/shard_map/psum | solution.py:17
  328.3 0.0 all-gather.9.cloned.1.call-done
  328.4 0.0 copy-done.6
  328.4 2.0 fusion.4
  330.4 1.6 tile.2
  332.0 10.2 %all-to-all-start = ((bf16[1024,64,16]{0,2,1:T(8,128)(2,1)}), bf16[1024,64,16]{0,2,1:T(8,128)(2,1)S(1)}, u32[]{:S(2)}, u32[]{:S(2)}) async-start(bf16[1024,64,16]{0,2,1:T(8,128)(2,1)} %tile.2), calls=%async_computation | async-start | bytes 4194304 | tf_op jit(solution)/shard_map/all_to_all | solution.py:10
  342.2 0.0 copy-start.4
  342.2 0.0 all-gather.11.cloned.1.call-start
  342.3 51.2 %all-to-all-done = bf16[1024,64,16]{0,2,1:T(8,128)(2,1)S(1)} async-done(((bf16[1024,64,16]{0,2,1:T(8,128)(2,1)}), bf16[1024,64,16]{0,2,1:T(8,128)(2,1)S(1)}, u32[]{:S(2)}, u32[]{:S(2)}) %all-to-all-start) | async-done | bytes 2097184 | tf_op jit(solution)/shard_map/all_to_all | solution.py:10
  393.5 1.8 convolution_convert_fusion
  395.3 0.0 all-gather.11.cloned.1.call-update
  395.3 0.0 all-reduce.3.cloned.1.call-start
  395.3 0.0 slice-start
  395.4 2.4 fusion.2
  397.8 0.3 fusion.5
  398.1 24.9 %all_gather.27 = bf16[1024,128]{1,0:T(8,128)(2,1)S(1)} all-gather(bf16[128,128]{1,0:T(8,128)(2,1)S(1)} %fusion.5), channel_id=1, replica_groups=mesh['row'=8,'col'=16,'vox'=4] {'row'}, dimensions={0}, use_global_device_ids=true | all-gather | bytes 294912 | tf_op jit(solution)/shard_map/all_gather | solution.py:79
  423.0 0.7 fusion.3
  423.7 0.8 pad_maximum_fusion
  424.6 0.0 copy-done
  424.6 0.8 dynamic-slice_select_fusion.1
  425.4 0.7 convolution_subtract_fusion.1
  426.1 45.2 %all-gather.11.cloned.1.call-done = bf16[1024,1024]{0,1:T(8,128)(2,1)} async-done(((bf16[1024,16]{0,1:T(8,128)(2,1)}), bf16[1024,1024]{0,1:T(8,128)(2,1)}) %all-gather.11.cloned.1.call-update) | async-done | bytes 2097168 | tf_op jit(solution)/shard_map/all_gather | solution.py:58
  471.4 1.7 dynamic-slice_select_fusion
  473.1 0.0 all-reduce.3.cloned.1.call-update
  473.1 0.8 dynamic-slice_bitcast_fusion.3
  473.9 0.6 pad_maximum_fusion.1
  474.5 3.2 convolution_subtract_fusion
  477.7 75.4 %all-reduce.3.cloned.1.call-done = (bf16[128,1024]{0,1:T(8,128)(2,1)}, bf16[128,1024]{0,1:T(8,128)(2,1)}) async-done(((bf16[128,1024]{0,1:T(8,128)(2,1)}, bf16[128,1024]{0,1:T(8,128)(2,1)}), (bf16[128,1024]{0,1:T(8,128)(2,1)}, bf16[128,1024]{0,1:T(8,128)(2,1)})) %all-reduce.3.cloned.1.call-update) | async-done | bytes 524304 | tf_op jit(solution)/shard_map/psum | solution.py:17
  553.0 1.8 convolution_subtract_fusion.3
  554.9 0.0 copy-done.1
  554.9 0.0 copy-done.5
  554.9 1.5 convolution_subtract_fusion.2
  (12 shorter events, 0.0 us)
Async XLA Ops:
  7.2 152.4 %copy-start.7 = (bf16[128,16]{0,1:T(8,128)(2,1)S(1)}, bf16[128,16]{0,1:T(8,128)(2,1)}, u32[]{:S(2)}) copy-start(bf16[128,16]{0,1:T(8,128)(2,1)} %param.7) | copy-start | bytes 12292
  7.2 90.2 %all-gather.7.cloned.1.call-start = ((), (), s32[]{:S(2)}) async-start(), calls=%async_computation.2 | async-start | bytes 2129920 | tf_op jit(solution)/shard_map/all_gather | solution.py:38
  7.9 149.0 %all-gather.5.cloned.1.call-start = ((), (), s32[]{:S(2)}) async-start(), calls=%async_computation.1 | async-start | bytes 4718592 | tf_op jit(solution)/shard_map/all_gather | solution.py:34
  8.7 319.7 %copy-start.6 = (bf16[1024,16]{0,1:T(8,128)(2,1)S(1)}, bf16[1024,16]{0,1:T(8,128)(2,1)}, u32[]{:S(2)}) copy-start(bf16[1024,16]{0,1:T(8,128)(2,1)} %param.9) | copy-start | bytes 98308
  8.7 319.7 %all-gather.9.cloned.1.call-start = ((), (), s32[]{:S(2)}) async-start(), calls=%async_computation.3 | async-start | bytes 2129920 | tf_op jit(solution)/shard_map/all_gather | solution.py:41
  332.0 61.5 %all-to-all-start = ((bf16[1024,64,16]{0,2,1:T(8,128)(2,1)}), bf16[1024,64,16]{0,2,1:T(8,128)(2,1)S(1)}, u32[]{:S(2)}, u32[]{:S(2)}) async-start(bf16[1024,64,16]{0,2,1:T(8,128)(2,1)} %tile.2), calls=%async_computation | async-start | bytes 4194304 | tf_op jit(solution)/shard_map/all_to_all | solution.py:10
  342.2 53.1 %copy-start.4 = (bf16[2,1024,128]{2,1,0:T(8,128)(2,1)S(1)}, bf16[2,1024,128]{2,1,0:T(8,128)(2,1)}, u32[]{:S(2)}) copy-start(bf16[2,1024,128]{2,1,0:T(8,128)(2,1)} %param.12) | copy-start | bytes 1572868
  342.2 129.1 %all-gather.11.cloned.1.call-start = ((), (), s32[]{:S(2)}) async-start(), calls=%async_computation.4 | async-start | bytes 2129920 | tf_op jit(solution)/shard_map/all_gather | solution.py:58
  395.3 157.7 %all-reduce.3.cloned.1.call-start = ((), (), s32[]{:S(2)}) async-start(), calls=%async_computation.5 | async-start | bytes 1048576 | tf_op jit(solution)/shard_map/psum | solution.py:17
  395.3 2.5 slice-start
  395.4 27.6 %copy-start.8 = (bf16[2,1024,1024]{2,1,0:T(8,128)(2,1)S(1)}, bf16[2,1024,1024]{2,1,0:T(8,128)(2,1)}, u32[]{:S(2)}) copy-start(bf16[2,1024,1024]{2,1,0:T(8,128)(2,1)} %all-gather.5.cloned.1.call-done) | copy-start | bytes 12582916
  423.0 1.6 copy-start
  423.0 2.4 copy-start.2
  474.5 78.5 %copy-start.3 = (bf16[1024,128]{1,0:T(8,128)(2,1)S(1)}, bf16[1024,128]{1,0:T(8,128)(2,1)}, u32[]{:S(2)}) copy-start(bf16[1024,128]{1,0:T(8,128)(2,1)} %param.10) | copy-start | bytes 786436
  553.0 1.8 copy-start.1
  553.0 1.9 copy-start.5
Sparse Core Ops, SparseCore 0:
  11.4 85.9 all-gather.6
  99.5 57.3 all-gather.4
  160.8 79.3 all-gather.8
  395.4 75.9 all-gather.10
  474.1 78.8 all-reduce.2
